TPU v7x, 32 devices: a whole 2x2x4 slice. The times are simulated.
32 devices in a mesh: wide: 16 (over z, x, core), narrow: 2 (over y).
Axes of the slice: x: 2, y: 2, z: 4, core: 2. Of those that a mesh axis runs over, the one named last changes fastest.
Arguments:
- activations: bfloat16 [4096, 8192], P('narrow', 'wide'), may hold values from -6 to 6
- cotangent: bfloat16 [4096, 4096], P('wide', 'narrow'), may hold values from -6 to 6
- sign_bits: int32 [8192, 4096], P('wide', 'narrow'), may hold values from 0 to 1
- seg_lengths: int32 [4], replicated, may hold values from 1 to 1536, 4096 in all
- kept_index: int32 [16384], replicated, may hold values from 0 to 33554431
Outputs:
- sketch: float32 [4, 16384], P(None, ('wide', 'narrow'))
Inputs may be any that keep to these rules, and one draw needn't show every extreme that they name: `seg_lengths`: the lengths sum to 4096; the longest is exactly 1536.
All inputs are finite; a program needn't handle non-finite values.
Results may differ from a plain program's by a relative error of at most 0.0003.
Values may be sent and summed in bfloat16 or wider, within the bound.
A program may use at most 192 MiB of HBM per device.

v0:
```python
import math

import jax
import jax.numpy as jnp
from jax import lax
from jax.sharding import PartitionSpec as P

MOST = 1536


def sylvester(extent):
    indices = jnp.arange(extent, dtype=jnp.int32)
    common = indices[:, None] & indices[None, :]
    parity = jnp.zeros((extent, extent), jnp.int32)
    for bit_pos in range(extent.bit_length() - 1):
        parity = parity + (common >> bit_pos & 1)
    return (1 - 2 * (parity % 2)).astype(jnp.float32)


def body(activations, cotangent, sign_bits, seg_lengths, kept_index):
    highest = lax.Precision.HIGHEST
    all_acts = lax.all_gather(activations, "narrow", axis=0, tiled=True)
    all_cots = lax.all_gather(cotangent, "wide", axis=0, tiled=True)
    total_tok = all_acts.shape[0]
    rows_local, cols_local = sign_bits.shape
    wide_count = lax.axis_size("wide")
    narrow_count = lax.axis_size("narrow")
    seg_count = seg_lengths.shape[0]
    starts = jnp.cumsum(seg_lengths) - seg_lengths

    def segment_grad(packed):
        begin_at, count = packed
        clamped = jnp.minimum(begin_at, total_tok - MOST)
        rows_x = lax.dynamic_slice_in_dim(all_acts, clamped, MOST, 0)
        rows_c = lax.dynamic_slice_in_dim(all_cots, clamped, MOST, 0)
        where_at = clamped + jnp.arange(MOST, dtype=jnp.int32)
        inside = (where_at >= begin_at) & (where_at < begin_at + count)
        rows_c = jnp.where(inside[:, None], rows_c, jnp.zeros((), jnp.bfloat16))
        grad = lax.dot_general(
            rows_x, rows_c, (((0,), (0,)), ((), ())), preferred_element_type=jnp.float32
        )
        return grad * lax.rsqrt(count.astype(jnp.float32))

    grads = lax.map(segment_grad, (starts, seg_lengths))
    signed = grads * (1 - 2 * sign_bits).astype(jnp.float32)[None]
    mixed = jnp.einsum("ab,sbc->sac", sylvester(rows_local), signed, precision=highest)
    mixed = jnp.einsum("sac,cd->sad", mixed, sylvester(cols_local), precision=highest)
    scale = 1.0 / math.sqrt(rows_local * wide_count * cols_local * narrow_count)
    full_cols = cols_local * narrow_count
    row_of = kept_index // full_cols
    col_of = kept_index % full_cols
    local_row = row_of % rows_local
    wide_sign = jnp.take(sylvester(wide_count), row_of // rows_local, axis=0)
    wide_sign = jnp.take(wide_sign, lax.axis_index("wide"), axis=1)
    narrow_sign = jnp.take(sylvester(narrow_count), col_of // cols_local, axis=0)
    narrow_sign = jnp.take(narrow_sign, lax.axis_index("narrow"), axis=1)
    local_flat = local_row * cols_local + col_of % cols_local
    picked = jnp.take(mixed.reshape(seg_count, -1), local_flat, axis=1)
    picked = picked * (wide_sign * narrow_sign * scale)[None, :]
    return lax.psum_scatter(picked, ("wide", "narrow"), scatter_dimension=1, tiled=True)


def solution(mesh):
    return jax.shard_map(
        body,
        mesh=mesh,
        in_specs=(P("narrow", "wide"), P("wide", "narrow"), P("wide", "narrow"), P(), P()),
        out_specs=P(None, ("wide", "narrow")),
        check_vma=False,
    )
```

profile of v0, /device:TPU:0, one launch (start us, length us, event | category | flops | bytes accessed | tf_op | source)
XLA Modules:
  0.0 829.1 jit_solution(16921129572293711092)
XLA Ops:
  6.5 0.0 all-gather.3.cloned.1.call-start
  6.5 0.7 all-gather.3.cloned.1.call-update
  7.3 0.0 all-gather.5.cloned.1.call-start
  7.3 0.7 all-gather.5.cloned.1.call-update
  8.0 0.0 reduce-scatter.4.cloned.1.call-start
  8.1 0.8 reduce-window.9
  8.9 1.7 compare_and_fusion.1
  10.6 54.5 %gather_fusion.2 = f32[16384,2]{1,0:T(8,128)} fusion(f32[2,2]{1,0:T(2,128)S(1)} %fusion.80, s32[16384]{0:T(1024)S(1)} %get-tuple-element.82), kind=kCustom, calls=%fused_computation.2 | custom fusion | bytes 327680 | tf_op jit(solution)/shard_map/jit(_take)/gather | solution.py:55
  65.1 0.0 copy-start.1
  65.1 54.5 %gather_fusion.1 = f32[16384,16]{1,0:T(8,128)} fusion(f32[16,16]{1,0:T(8,128)S(1)} %fusion.77, s32[16384]{0:T(1024)S(1)} %get-tuple-element.83), kind=kCustom, calls=%fused_computation.1 | custom fusion | bytes 2162688 | tf_op jit(solution)/shard_map/jit(_take)/gather | solution.py:53
  119.6 0.0 copy-done.1
  119.6 5.1 subtract_convert_fusion
  124.7 13.8 %fusion.29 = f32[16384]{0:T(1024)S(1)} fusion(f32[16384,2]{1,0:T(8,128)} %gather_fusion.2, s32[]{:T(128)S(6)} %select_n.120, f32[16384,16]{1,0:T(8,128)} %gather_fusion.1, s32[]{:T(128)S(6)} %select_n.114, pred[16384]{0:T(1024)(128)(4,1)S(1)} %get-tuple-element.78, pred[16384]{0:T(1024)(128)(4,1)S(1)} %get-tuple-element.74, pred[]{:T(512)S(6)} %and.258, ...), kind=kLoop, calls=%fused_computation.35 | loop fusion | flops 98304 | bytes 229386 | tf_op jit(solution)/shard_map/mul | solution.py:59
  138.5 26.2 %fusion.105 = f32[2048,2048,1]{1,0,2:T(8,128)} fusion(), kind=kLoop, calls=%fused_computation.23.clone.clone.clone.clone.1 | loop fusion | flops 197132288 | bytes 16777216 | tf_op jit(solution)/shard_map/sac,cd->sad/dot_general | solution.py:47
  164.8 0.0 all-gather.3.cloned.1.call-done
  164.8 32.2 %all-gather.5.cloned.1.call-done = bf16[4096,2048]{1,0:T(8,128)(2,1)} async-done(((bf16[256,2048]{1,0:T(8,128)(2,1)}), bf16[4096,2048]{1,0:T(8,128)(2,1)}) %all-gather.5.cloned.1.call-update) | async-done | bytes 16777232 | tf_op jit(solution)/shard_map/all_gather | solution.py:23
  197.0 52.4 %while.12 = (s32[]{:T(128)}, f32[4,512,2048]{2,1,0:T(8,128)}, s32[4]{0:T(128)S(1)}, bf16[4096,512]{1,0:T(8,128)(2,1)}, s32[4]{0:T(128)S(1)}, /*index=5*/bf16[409...) while((s32[]{:T(128)}, f32[4,512,2048]{2,1,0:T(8,128)}, s32[4]{0:T(128)S(1)}, ...), condition=%wide.region_2.3_spmd, body=%wide.region_1.2_spmd.sunk | while | flops 3225425920 | bytes 12063963 | solution.py:44
  197.0 0.6 dynamic_slice.27
  198.2 0.6 dynamic_slice.28
  199.9 0.6 fusion.112
  201.1 9.0 %bitcast_dynamic-update-slice_fusion.2 = f32[4,512,2048]{2,1,0:T(8,128)} fusion(f32[4,512,2048]{2,1,0:T(8,128)} %get-tuple-element.132, s32[]{:T(128)S(6)} %copy.16, bf16[4096,2048]{1,0:T(8,128)(2,1)} %get-tuple-element.146, s32[]{:T(128)S(6)} %select_n.242, pred[1536]{0:T(1024)(128)(4,1)S(1)} %fusion.112, f32[]{:T(128)S(6)} %rsqrt.4, ...), kind=kOutput, calls=%fused_computation.7.clone.1 | convolution fusion | flops 3225419776 | bytes 12062208 | tf_op jit(solution)/shard_map/while/body/eval_jaxpr/dot_general | solution.py:39
  210.2 0.6 dynamic_slice.27
  211.4 0.6 dynamic_slice.28
  213.1 0.6 fusion.112
  214.3 8.9 %bitcast_dynamic-update-slice_fusion.2 = f32[4,512,2048]{2,1,0:T(8,128)} fusion(f32[4,512,2048]{2,1,0:T(8,128)} %get-tuple-element.132, s32[]{:T(128)S(6)} %copy.16, bf16[4096,2048]{1,0:T(8,128)(2,1)} %get-tuple-element.146, s32[]{:T(128)S(6)} %select_n.242, pred[1536]{0:T(1024)(128)(4,1)S(1)} %fusion.112, f32[]{:T(128)S(6)} %rsqrt.4, ...), kind=kOutput, calls=%fused_computation.7.clone.1 | convolution fusion | flops 3225419776 | bytes 12062208 | tf_op jit(solution)/shard_map/while/body/eval_jaxpr/dot_general | solution.py:39
  223.2 0.6 dynamic_slice.27
  224.5 0.6 dynamic_slice.28
  226.2 0.6 fusion.112
  227.4 8.9 %bitcast_dynamic-update-slice_fusion.2 = f32[4,512,2048]{2,1,0:T(8,128)} fusion(f32[4,512,2048]{2,1,0:T(8,128)} %get-tuple-element.132, s32[]{:T(128)S(6)} %copy.16, bf16[4096,2048]{1,0:T(8,128)(2,1)} %get-tuple-element.146, s32[]{:T(128)S(6)} %select_n.242, pred[1536]{0:T(1024)(128)(4,1)S(1)} %fusion.112, f32[]{:T(128)S(6)} %rsqrt.4, ...), kind=kOutput, calls=%fused_computation.7.clone.1 | convolution fusion | flops 3225419776 | bytes 12062208 | tf_op jit(solution)/shard_map/while/body/eval_jaxpr/dot_general | solution.py:39
  236.3 0.6 dynamic_slice.27
  237.5 0.6 dynamic_slice.28
  239.2 0.6 fusion.112
  240.4 8.9 %bitcast_dynamic-update-slice_fusion.2 = f32[4,512,2048]{2,1,0:T(8,128)} fusion(f32[4,512,2048]{2,1,0:T(8,128)} %get-tuple-element.132, s32[]{:T(128)S(6)} %copy.16, bf16[4096,2048]{1,0:T(8,128)(2,1)} %get-tuple-element.146, s32[]{:T(128)S(6)} %select_n.242, pred[1536]{0:T(1024)(128)(4,1)S(1)} %fusion.112, f32[]{:T(128)S(6)} %rsqrt.4, ...), kind=kOutput, calls=%fused_computation.7.clone.1 | convolution fusion | flops 3225419776 | bytes 12062208 | tf_op jit(solution)/shard_map/while/body/eval_jaxpr/dot_general | solution.py:39
  249.3 62.1 %fusion.21 = f32[4,2048,512]{2,1,0:T(8,128)} fusion(f32[4,512,2048]{2,1,0:T(8,128)} %get-tuple-element.37, f32[512,2048]{1,0:T(8,128)} %subtract_convert_fusion), kind=kOutput, calls=%fused_computation.26 | convolution fusion | flops 25784745984 | bytes 37748736 | tf_op jit(solution)/shard_map/ab,sbc->sac/dot_general | solution.py:46
  311.4 116.9 %fusion.43 = f32[1,4,512,2048]{3,2,1,0:T(8,128)} fusion(f32[4,2048,512]{2,1,0:T(8,128)} %fusion.21, f32[2048,2048,1]{1,0,2:T(8,128)} %fusion.105), kind=kOutput, calls=%fused_computation.50 | convolution fusion | flops 103079215104 | bytes 50331648 | tf_op jit(solution)/shard_map/sac,cd->sad/dot_general | solution.py:47
  428.4 20.9 %copy.12 = f32[1,4,512,2048]{3,1,2,0:T(4,128)} copy(f32[1,4,512,2048]{3,2,1,0:T(8,128)} %fusion.43) | data formatting | bytes 33554432
  449.3 0.0 copy-start
  449.3 184.6 %gather_fusion = f32[16384,4]{0,1:T(4,128)S(1)} fusion(f32[4,1048576]{1,0:T(4,128)} %bitcast.39, s32[16384]{0:T(1024)S(1)} %broadcast_clamp_fusion.2), kind=kCustom, calls=%fused_computation | custom fusion | bytes 589824 | tf_op jit(solution)/shard_map/jit(_take)/gather | solution.py:58
  633.9 0.0 copy-done
  633.9 0.1 multiply_bitcast_fusion
  634.1 5.1 copy.10
  639.1 0.0 reduce-scatter.4.cloned.1.call-update
  639.2 181.8 %reduce-scatter.4.cloned.1.call-done = f32[512,4]{1,0:T(8,128)} async-done(((f32[16384,4]{1,0:T(8,128)}), f32[512,4]{1,0:T(8,128)}) %reduce-scatter.4.cloned.1.call-update) | async-done | bytes 8208
  820.9 1.7 copy.11
  (6 shorter events, 0.1 us)
Async XLA Ops:
  6.5 158.2 %all-gather.3.cloned.1.call-start = ((), (), s32[]{:S(2)}) async-start(), calls=%async_computation.1 | async-start | bytes 6291456 | tf_op jit(solution)/shard_map/all_gather | solution.py:22
  7.3 189.7 %all-gather.5.cloned.1.call-start = ((), (), s32[]{:S(2)}) async-start(), calls=%async_computation.2 | async-start | bytes 17825792 | tf_op jit(solution)/shard_map/all_gather | solution.py:23
  8.0 812.9 %reduce-scatter.4.cloned.1.call-start = ((), (), s32[]{:S(2)}) async-start(), calls=%async_computation.3 | async-start | bytes 8650752
  65.1 54.5 %copy-start.1 = (s32[4]{0:T(128)S(1)}, s32[4]{0:T(128)}, u32[]{:S(2)}) copy-start(s32[4]{0:T(128)} %param.10) | copy-start | bytes 52
  449.3 184.6 %copy-start = (pred[16384]{0:T(1024)(128)(4,1)S(1)}, pred[16384]{0:T(1024)(128)(4,1)}, u32[]{:S(2)}) copy-start(pred[16384]{0:T(1024)(128)(4,1)} %get-tuple-element.80) | copy-start | bytes 49156
Sparse Core Ops, SparseCore 0:
  8.9 59.4 all-gather.2
  70.5 126.4 all-gather.4
  639.3 181.6 reduce-scatter.3
where the time goes:
time: 834 us; the launch traced here: 829 us
  local copies, waits for them, and re-layouts  326 us (39%)
  waiting for transfers between devices  215 us (26%)
  matrix products  215 us (26%)
  other arithmetic  50.3 us (6%)
  between operations  13.2 us (2%)
  loops' own time  9.46 us (1%)
    gather x1, local copies, waits for them, and re-layouts, body(): picked = jnp.take(mixed.reshape(seg_count, -1), local_flat, axis=1)  185 us
    unnamed x4, waiting for transfers between devices  183 us
    dot_general x1, matrix products, body(): jnp.einsum('sac,cd->sad', mixed, sylvester(cols_local), precision=highest)  117 us
    dot_general x1, matrix products, body(): jnp.einsum('ab,sbc->sac', sylvester(rows_local), signed, precision=highest)  62.1 us
    gather x1, local copies, waits for them, and re-layouts, body(): jnp.take(sylvester(narrow_count), col_of // cols_local, axis=0)  54.5 us
    gather x1, local copies, waits for them, and re-layouts, body(): wide_sign = jnp.take(sylvester(wide_count), row_of // rows_local, axis=0)  54.5 us
    dot_general x4, matrix products, segment_grad(): lax.dot_general(rows_x, rows_c, (((0,), (0,)), ((), ())), preferred_eleme...  35.8 us
    all_gather x1, waiting for transfers between devices, body(): all_cots = lax.all_gather(cotangent, 'wide', axis=0, tiled=True)  32.2 us
  transfers between devices with their start and end apart: 3, of which 2 were waited for; matrix products, arithmetic and copies ran while one was open for 19% of the time, Pallas kernels for 0%

commit v1 on v0

v1 whole, which is shorter than its diff:
```python
import functools
import math

import jax
import jax.numpy as jnp
import numpy as np
from jax import lax
from jax.experimental import pallas as pl
from jax.experimental.pallas import tpu as pltpu
from jax.sharding import PartitionSpec as P

LANES = 128
MESH = pl.DeviceIdType.MESH


def sylvester(extent):
    indices = np.arange(extent)
    common = indices[:, None] & indices[None, :]
    parity = np.zeros((extent, extent), np.int64)
    for bit_pos in range(extent.bit_length() - 1):
        parity += common >> bit_pos & 1
    return jnp.asarray(1 - 2 * (parity % 2), jnp.bfloat16)


def spread_kernel(
    n_wide, n_narrow, cross,
    acts, cots, acts_all, cots_all,
    acts_own, cots_own, local_sem, acts_send, acts_recv, cots_send, cots_recv,
):
    wide = lax.axis_index("wide")
    narrow = lax.axis_index("narrow")
    lines = n_wide // (2 * cross)
    core = lax.rem(wide, 2)
    side = lax.rem(wide // 2, cross)
    place = wide // (2 * cross)
    tok_acts = acts.shape[0]
    tok_cots = cots.shape[0]

    def index_of(at, across, on_core):
        return (at * cross + across) * 2 + on_core

    partner = index_of(place, side, 1 - core)
    up = index_of(lax.rem(place + 1, lines), side, core)
    down = index_of(lax.rem(place + lines - 1, lines), side, core)
    across = [lax.rem(side + off, cross) for off in range(1, cross)]
    has_up = place < lines - 1
    has_down = place > 0

    barrier = pltpu.get_barrier_semaphore()

    def greet(**where):
        pl.semaphore_signal(barrier, inc=1, device_id=where, device_id_type=MESH)

    greet(wide=partner)
    for other in across:
        greet(wide=index_of(place, other, core))
    for off in range(1, n_narrow):
        greet(narrow=lax.rem(narrow + off, n_narrow))

    @pl.when(has_up)
    def _():
        greet(wide=up)

    @pl.when(has_down)
    def _():
        greet(wide=down)

    ends = jnp.where(has_up, 1, 0) + jnp.where(has_down, 1, 0)
    pl.semaphore_wait(barrier, 1 + (cross - 1) + (n_narrow - 1) + ends)

    def acts_copy(off):
        return pltpu.make_async_remote_copy(
            src_ref=acts,
            dst_ref=acts_all.at[pl.ds(narrow * tok_acts, tok_acts), :],
            send_sem=acts_send.at[off],
            recv_sem=acts_recv.at[off],
            device_id={"narrow": lax.rem(narrow + off, n_narrow)},
            device_id_type=MESH,
        )

    def cots_copy(way, shard, to, own):
        window = pl.ds(shard * tok_cots, tok_cots)
        return pltpu.make_async_remote_copy(
            src_ref=cots if own else cots_all.at[window, :],
            dst_ref=cots_all.at[window, :],
            send_sem=cots_send.at[way, shard],
            recv_sem=cots_recv.at[shard],
            device_id={"wide": to},
            device_id_type=MESH,
        )

    def outgoing(shard, own, climbs, drops, crosses):
        todo = []
        if climbs:
            todo.append((has_up, cots_copy(0, shard, up, own)))
        if drops:
            todo.append((has_down, cots_copy(1, shard, down, own)))
        if crosses:
            for at, other in enumerate(across):
                to = index_of(place, other, core)
                todo.append((None, cots_copy(3 + at, shard, to, own)))
        todo.append((None, cots_copy(2, shard, partner, own)))
        return todo

    def each(todo, act):
        for condition, copy in todo:
            if condition is None:
                act(copy)
            else:
                pl.when(condition)(functools.partial(act, copy))

    def start(copy):
        copy.start()

    def sent(copy):
        copy.wait_send()

    def arrived(shard):
        cots_copy(2, shard, partner, False).wait_recv()

    mine = outgoing(wide, True, True, True, True)
    each(mine, start)
    for off in range(1, n_narrow):
        acts_copy(off).start()

    to_vmem = (
        pltpu.make_async_copy(acts, acts_own, local_sem.at[0]),
        pltpu.make_async_copy(cots, cots_own, local_sem.at[1]),
    )
    from_vmem = (
        pltpu.make_async_copy(
            acts_own, acts_all.at[pl.ds(narrow * tok_acts, tok_acts), :], local_sem.at[2]
        ),
        pltpu.make_async_copy(
            cots_own, cots_all.at[pl.ds(wide * tok_cots, tok_cots), :], local_sem.at[3]
        ),
    )
    for copy in to_vmem:
        copy.start()
    for copy, back in zip(to_vmem, from_vmem):
        copy.wait()
        back.start()

    def below(step):
        return place - step >= 0, index_of(place - step, side, core)

    def above(step):
        return place + step < lines, index_of(place + step, side, core)

    def crossed(step):
        for other in across:
            if step == 0:
                shard = index_of(place, other, core)
                arrived(shard)
                each(outgoing(shard, False, False, False, False), start)
                continue

            @pl.when(place - step >= 0)
            def _():
                shard = index_of(place - step, other, core)
                arrived(shard)
                each(outgoing(shard, False, False, False, False), start)

            @pl.when(place + step < lines)
            def _():
                shard = index_of(place + step, other, core)
                arrived(shard)
                each(outgoing(shard, False, False, False, False), start)

    for step in range(1, lines):
        there, shard_below = below(step)

        @pl.when(there)
        def _():
            arrived(shard_below)
            each(outgoing(shard_below, False, True, False, True), start)

        there, shard_above = above(step)

        @pl.when(there)
        def _():
            arrived(shard_above)
            each(outgoing(shard_above, False, False, True, True), start)

        crossed(step - 1)
    crossed(lines - 1)

    for at in range(lines):
        for over in range(cross):
            arrived(index_of(at, over, 1 - core))
    for off in range(1, n_narrow):
        acts_copy(off).wait()
    for copy in from_vmem:
        copy.wait()
    each(mine, sent)
    for step in range(1, lines):
        there, shard_below = below(step)

        @pl.when(there)
        def _():
            each(outgoing(shard_below, False, True, False, True), sent)

        there, shard_above = above(step)

        @pl.when(there)
        def _():
            each(outgoing(shard_above, False, False, True, True), sent)

    for at in range(lines):
        for other in across:
            shard = index_of(at, other, core)
            each(outgoing(shard, False, False, False, False), sent)


def spread(acts, cots, n_wide, n_narrow):
    cross = 2
    anywhere = pl.BlockSpec(memory_space=pl.ANY)
    return pl.pallas_call(
        functools.partial(spread_kernel, n_wide, n_narrow, cross),
        out_shape=(
            jax.ShapeDtypeStruct((acts.shape[0] * n_narrow, acts.shape[1]), acts.dtype),
            jax.ShapeDtypeStruct((cots.shape[0] * n_wide, cots.shape[1]), cots.dtype),
        ),
        in_specs=[anywhere, anywhere],
        out_specs=(anywhere, anywhere),
        scratch_shapes=[
            pltpu.VMEM(acts.shape, acts.dtype),
            pltpu.VMEM(cots.shape, cots.dtype),
            pltpu.SemaphoreType.DMA((4,)),
            pltpu.SemaphoreType.DMA((n_narrow,)),
            pltpu.SemaphoreType.DMA((n_narrow,)),
            pltpu.SemaphoreType.DMA((2 + cross, n_wide)),
            pltpu.SemaphoreType.DMA((n_wide,)),
        ],
        compiler_params=pltpu.CompilerParams(collective_id=0, has_side_effects=True),
        name="spread",
    )(acts, cots)


def butterflies(parts):
    parts = list(parts)
    gap = 1
    while gap < len(parts):
        for low in range(len(parts)):
            if not low & gap:
                one, two = parts[low], parts[low | gap]
                parts[low], parts[low | gap] = one + two, one - two
        gap *= 2
    return parts


def halves(values):
    high = values.astype(jnp.bfloat16)
    low = (values - high.astype(jnp.float32)).astype(jnp.bfloat16)
    return high, low


def sketch_kernel(
    seg_count, steps_ref, spots_ref, gains_ref,
    acts_ref, cots_ref, bits_ref, left_ref, right_ref, signs_ref,
    out_ref, flipped, total, table,
):
    step = pl.program_id(0)
    tile = steps_ref[0, step]
    seg = steps_ref[1, step]
    first = steps_ref[2, step]
    last = steps_ref[3, step]
    low = steps_ref[4, step]
    high = steps_ref[5, step]
    tok = acts_ref.shape[0]
    rows, cols = bits_ref.shape
    row_block = left_ref.shape[0]
    col_block = right_ref.shape[0]
    row_groups = rows // row_block
    col_groups = cols // col_block

    @pl.when(low < high)
    def _():
        where_at = tile * tok + lax.broadcasted_iota(jnp.int32, acts_ref.shape, 0)
        inside = (where_at >= low) & (where_at < high)
        values = jnp.where(inside, acts_ref[...].astype(jnp.float32), 0.0)
        flipped[...] = values.T.astype(jnp.bfloat16)

        def columns(at, _):
            window = pl.ds(pl.multiple_of(at * col_block, col_block), col_block)
            grad = jnp.dot(
                flipped[...], cots_ref[:, window], preferred_element_type=jnp.float32
            )

            @pl.when(first == 1)
            def _():
                total[:, window] = grad

            @pl.when(first == 0)
            def _():
                total[:, window] += grad

            return 0

        lax.fori_loop(0, col_groups, columns, 0)

    @pl.when(last == 1)
    def _():
        gain = gains_ref[seg]

        def columns(at, _):
            window = pl.ds(pl.multiple_of(at * col_block, col_block), col_block)
            parts = []
            for group in range(row_groups):
                part = pl.ds(group * row_block, row_block)
                sign = (1 - 2 * bits_ref[part, window]).astype(jnp.float32)
                parts.append(total[part, window] * (sign * gain))
            for group, part in enumerate(butterflies(parts)):
                upper, lower = halves(part)
                mixed = jnp.dot(
                    left_ref[...], upper, preferred_element_type=jnp.float32
                ) + jnp.dot(left_ref[...], lower, preferred_element_type=jnp.float32)
                upper, lower = halves(mixed)
                mixed = jnp.dot(
                    upper, right_ref[...], preferred_element_type=jnp.float32
                ) + jnp.dot(lower, right_ref[...], preferred_element_type=jnp.float32)
                total[pl.ds(group * row_block, row_block), window] = mixed
            return 0

        lax.fori_loop(0, col_groups, columns, 0)
        per_group = col_block // LANES

        def across(at, _):
            base = pl.multiple_of(at * 8, 8)
            for lane_block in range(per_group):
                parts = [
                    total[pl.ds(base, 8), pl.ds(group * col_block + lane_block * LANES, LANES)]
                    for group in range(col_groups)
                ]
                for group, part in enumerate(butterflies(parts)):
                    block = group * per_group + lane_block
                    begin = (block * rows + base) * seg_count + seg
                    table[pl.ds(begin, 8, stride=seg_count), :] = part
            return 0

        lax.fori_loop(0, rows // 8, across, 0)

    @pl.when(step == pl.num_programs(0) - 1)
    def _():
        lane = lax.broadcasted_iota(jnp.int32, (8, LANES), 1)
        chains = 4

        def pick(group, _):
            found = [jnp.zeros((8, LANES), jnp.float32)] * chains
            for at in range(LANES):
                spot = spots_ref[group * LANES + at]
                values = table[pl.ds(lax.shift_right_logical(spot, 7), 8), :]
                values = pltpu.roll(values, spot & (LANES - 1), 1)
                found[at % chains] = jnp.where(lane == at, values, found[at % chains])
            both = (found[0] + found[1]) + (found[2] + found[3])
            out_ref[group] = both[:seg_count] * signs_ref[pl.ds(group, 1), :]
            return 0

        lax.fori_loop(0, out_ref.shape[0], pick, 0)


def local_sketch(acts, cots, bits, lengths, spots, signs):
    tokens = acts.shape[0]
    rows, cols = bits.shape
    seg_count = lengths.shape[0]
    groups = signs.shape[0]
    tok = 256
    row_block, col_block = min(rows, 256), min(cols, 256)
    steps = tokens // tok + seg_count - 1
    ends = jnp.cumsum(lengths)
    starts = ends - lengths
    first_tile = starts // tok
    tiles = (ends + tok - 1) // tok - first_tile
    after = jnp.cumsum(tiles)
    before = after - tiles
    at = jnp.arange(steps, dtype=jnp.int32)
    seg = jnp.sum((at[:, None] >= after[None, :-1]).astype(jnp.int32), axis=1)
    mine = (seg[:, None] == jnp.arange(seg_count)[None, :]).astype(jnp.int32)

    def of(values):
        return jnp.sum(mine * values[None, :], axis=1)

    begun = of(before)
    tile = jnp.minimum(of(first_tile) + at - begun, tokens // tok - 1)
    live = at < after[-1]
    low = jnp.where(live, of(starts), 0)
    high = jnp.where(live, of(ends), 0)
    table = jnp.stack(
        [
            tile,
            seg,
            (at == begun).astype(jnp.int32),
            (at == of(after) - 1).astype(jnp.int32),
            low,
            high,
        ]
    ).astype(jnp.int32)
    gains = lax.rsqrt(lengths.astype(jnp.float32))
    fixed = lambda i, *_: (0, 0)
    return pl.pallas_call(
        functools.partial(sketch_kernel, seg_count),
        out_shape=jax.ShapeDtypeStruct((groups, seg_count, LANES), jnp.float32),
        grid_spec=pltpu.PrefetchScalarGridSpec(
            num_scalar_prefetch=3,
            grid=(steps,),
            in_specs=[
                pl.BlockSpec((tok, rows), lambda i, t, *_: (t[0, i], 0)),
                pl.BlockSpec((tok, cols), lambda i, t, *_: (t[0, i], 0)),
                pl.BlockSpec((rows, cols), fixed),
                pl.BlockSpec((row_block, row_block), fixed),
                pl.BlockSpec((col_block, col_block), fixed),
                pl.BlockSpec(signs.shape, fixed),
            ],
            out_specs=pl.BlockSpec((groups, seg_count, LANES), lambda i, *_: (0, 0, 0)),
            scratch_shapes=[
                pltpu.VMEM((rows, tok), jnp.bfloat16),
                pltpu.VMEM((rows, cols), jnp.float32),
                pltpu.VMEM((rows * cols // LANES * seg_count + 8, LANES), jnp.float32),
            ],
        ),
        compiler_params=pltpu.CompilerParams(vmem_limit_bytes=60 * 1024 * 1024),
        name="local_sketch",
    )(table, spots, gains, acts, cots, bits, sylvester(row_block), sylvester(col_block), signs)


def add_up_kernel(n_wide, n_narrow, shares, out, held, send_sem, recv_sem):
    count = n_wide * n_narrow
    me = lax.axis_index("wide") * n_narrow + lax.axis_index("narrow")
    barrier = pltpu.get_barrier_semaphore()

    def address(who):
        return {"wide": who // n_narrow, "narrow": lax.rem(who, n_narrow)}

    def greet(off, _):
        who = lax.rem(me + off, count)
        pl.semaphore_signal(barrier, inc=1, device_id=address(who), device_id_type=MESH)
        return 0

    lax.fori_loop(1, count, greet, 0)
    pl.semaphore_wait(barrier, count - 1)

    def copy_to(who, slot):
        return pltpu.make_async_remote_copy(
            src_ref=shares.at[who],
            dst_ref=held.at[slot],
            send_sem=send_sem.at[who],
            recv_sem=recv_sem.at[slot],
            device_id=address(who),
            device_id_type=MESH,
        )

    def send(off, _):
        copy_to(lax.rem(me + off, count), me).start()
        return 0

    lax.fori_loop(1, count, send, 0)
    out[...] = shares[me]

    def take(off, _):
        who = lax.rem(me + count - off, count)
        copy_to(who, who).wait_recv()
        out[...] += held[who]
        return 0

    lax.fori_loop(1, count, take, 0)

    def sent(off, _):
        copy_to(lax.rem(me + off, count), me).wait_send()
        return 0

    lax.fori_loop(1, count, sent, 0)


def add_up(shares, n_wide, n_narrow):
    count = n_wide * n_narrow
    in_vmem = pl.BlockSpec(memory_space=pltpu.VMEM)
    return pl.pallas_call(
        functools.partial(add_up_kernel, n_wide, n_narrow),
        out_shape=jax.ShapeDtypeStruct(shares.shape[1:], shares.dtype),
        in_specs=[in_vmem],
        out_specs=in_vmem,
        scratch_shapes=[
            pltpu.VMEM(shares.shape, shares.dtype),
            pltpu.SemaphoreType.DMA((count,)),
            pltpu.SemaphoreType.DMA((count,)),
        ],
        compiler_params=pltpu.CompilerParams(collective_id=1, has_side_effects=True),
        name="add_up",
    )(shares)


def body(n_wide, n_narrow, activations, cotangent, sign_bits, seg_lengths, kept_index):
    rows, cols = sign_bits.shape
    seg_count = seg_lengths.shape[0]
    kept = kept_index.shape[0]
    count = n_wide * n_narrow
    all_acts, all_cots = spread(activations, cotangent, n_wide, n_narrow)

    scale = 1.0 / math.sqrt(rows * n_wide * cols * n_narrow)
    full_cols = cols * n_narrow
    row_of = kept_index // full_cols
    col_of = kept_index % full_cols
    common = lax.population_count((row_of // rows) & lax.axis_index("wide"))
    common = common + lax.population_count((col_of // cols) & lax.axis_index("narrow"))
    signs = (1 - 2 * (common & 1)).astype(jnp.float32) * scale
    col = col_of % cols
    row = ((col // LANES) * rows + row_of % rows) * seg_count
    lane = jnp.arange(kept, dtype=jnp.int32)
    spots = row * LANES + ((lane - col) & (LANES - 1))
    shares = local_sketch(
        all_acts, all_cots, sign_bits, seg_lengths, spots, signs.reshape(-1, LANES)
    )
    each = kept // count
    if each % LANES:
        flat = shares.transpose(1, 0, 2).reshape(seg_count, kept)
        return lax.psum_scatter(flat, ("wide", "narrow"), scatter_dimension=1, tiled=True)
    mine = add_up(shares.reshape(count, -1, LANES), n_wide, n_narrow)
    mine = mine.reshape(each // LANES, seg_count, LANES)
    return mine.transpose(1, 0, 2).reshape(seg_count, each)


def solution(mesh):
    return jax.shard_map(
        functools.partial(body, mesh.shape["wide"], mesh.shape["narrow"]),
        mesh=mesh,
        in_specs=(P("narrow", "wide"), P("wide", "narrow"), P("wide", "narrow"), P(), P()),
        out_specs=P(None, ("wide", "narrow")),
        check_vma=False,
    )
```

time: 834 us -> 231 us (0.28)
  local copies, waits for them, and re-layouts: 326 us -> 2.49 us
  Pallas kernels: 0 us -> 219 us
  matrix products: 215 us -> 0 us
  waiting for transfers between devices: 215 us -> 0 us
  other arithmetic: 50.3 us -> 6.98 us
  between operations: 13.2 us -> 0.05 us
  loops' own time: 9.46 us -> 0 us
    gather x3 -> x0, local copies, waits for them, and re-layouts: 294 us -> none  [the longest x1 185 us: body(): picked = jnp.take(mixed.reshape(seg_count, -1), local_flat, axis=1)]
    pallas_call x0 -> x3, Pallas kernels: none -> 219 us  [the longest x1 106 us: local_sketch(): pl.pallas_call(functools.partial(sketch_kernel, seg_count), out_shape=jax...]
    dot_general x6 -> x0, matrix products: 215 us -> none  [the longest x1 117 us: body(): jnp.einsum('sac,cd->sad', mixed, sylvester(cols_local), precision=highest)]
    unnamed x4 -> x0, waiting for transfers between devices: 183 us -> none
    all_gather x2 -> x0, waiting for transfers between devices: 32.2 us -> none  [the longest x1 32.2 us: body(): all_cots = lax.all_gather(cotangent, 'wide', axis=0, tiled=True)]
    unnamed x7 -> x1, local copies, waits for them, and re-layouts: 27.6 us -> 1.3 us
    dot_general x1 -> x0, other arithmetic: 26.2 us -> none  [body(): jnp.einsum('sac,cd->sad', mixed, sylvester(cols_local), precision=highest)]
    mul x2 -> x0, other arithmetic: 13.9 us -> none  [body(): picked = picked * (wide_sign * narrow_sign * scale)[None, :]]
  transfers between devices with their start and end apart: 3 -> 0, of which waited for: 2 -> 0; matrix products, arithmetic and copies ran while one was open for 19% -> 0% of each run, Pallas kernels for 0% -> 0%
where the time goes in v1:
time: 231 us; the launch traced here: 228 us
  Pallas kernels  219 us (95%)
  other arithmetic  6.98 us (3%)
  local copies, waits for them, and re-layouts  2.49 us (1%)
    pallas_call x1, Pallas kernels, local_sketch(): pl.pallas_call(functools.partial(sketch_kernel, seg_count), out_shape=jax...  106 us
    pallas_call x1, Pallas kernels, spread(): pl.pallas_call(functools.partial(spread_kernel, n_wide, n_narrow, cross),...  102 us
    pallas_call x1, Pallas kernels, add_up(): pl.pallas_call(functools.partial(add_up_kernel, n_wide, n_narrow), out_sh...  11 us

profile of v1, /device:TPU:0, one launch (start us, length us, event | category | flops | bytes accessed | tf_op | source)
XLA Modules:
  0.0 228.4 jit_solution(13361791984140331164)
XLA Ops:
  0.0 0.8 reduce-window.13
  0.8 1.2 convert_rsqrt_fusion.gains_ref
  2.1 0.7 fusion.24
  2.7 0.2 reduce-window.14
  2.9 0.6 slice.9
  3.5 0.1 convert_reduce_fusion
  3.6 0.1 select_reduce_fusion
  3.7 0.6 compare_select_fusion.6
  4.4 0.6 stack.5.steps_ref
  5.0 1.6 fusion.13.signs_ref
  6.6 1.6 fusion.4.spots_ref
  8.2 101.9 %spread.1 = (bf16[4096,512]{1,0:T(8,128)(2,1)}, bf16[4096,2048]{1,0:T(8,128)(2,1)}) custom-call(bf16[2048,512]{1,0:T(8,128)(2,1)} %acts.1, bf16[256,2048]{1,0:T(8,128)(2,1)} %cots.1), custom_call_target="tpu_custom_call" | custom-call | tf_op jit(solution)/shard_map/spread/pallas_call | solution.py:218
  110.1 106.0 %local_sketch.1 = f32[128,4,128]{2,1,0:T(4,128)} custom-call(s32[6,19]{1,0:T(8,128)} %stack.5.steps_ref, s32[16384]{0:T(1024)} %fusion.4.spots_ref, f32[4]{0:T(128)} %convert_rsqrt_fusion.gains_ref, bf16[4096,512]{1,0:T(8,128)(2,1)} %get-tuple-element.7.acts_ref, bf16[4096,2048]{1,0:T(8,128)(2,1)} %get-tuple-element.8.cots_ref, s32[512,2048]{1,0:T(8,128)} %bits_ref.1, ...), custom_call_target="tpu_custom_call" | custom-call | tf_op jit(solution)/shard_map/local_sketch/pallas_call | solution.py:400
  216.2 11.0 %add_up.1 = f32[16,128]{1,0:T(8,128)} custom-call(f32[32,16,128]{2,1,0:T(8,128)} %bitcast.35), custom_call_target="tpu_custom_call" | custom-call | tf_op jit(solution)/shard_map/add_up/pallas_call | solution.py:477
  227.1 1.3 copy.11
  (4 shorter events, 0.0 us)

commit v2 on v0

v2 whole, which is shorter than its diff:
```python
import functools
import math

import jax
import jax.numpy as jnp
import numpy as np
from jax import lax
from jax.experimental import pallas as pl
from jax.experimental.pallas import tpu as pltpu
from jax.sharding import PartitionSpec as P

LANES = 128
MOST = 1536
MESH = pl.DeviceIdType.MESH


def sylvester(extent):
    indices = np.arange(extent)
    common = indices[:, None] & indices[None, :]
    parity = np.zeros((extent, extent), np.int64)
    for bit_pos in range(extent.bit_length() - 1):
        parity += common >> bit_pos & 1
    return jnp.asarray(1 - 2 * (parity % 2), jnp.bfloat16)


def butterflies(parts):
    parts = list(parts)
    gap = 1
    while gap < len(parts):
        for low in range(len(parts)):
            if not low & gap:
                one, two = parts[low], parts[low | gap]
                parts[low], parts[low | gap] = one + two, one - two
        gap *= 2
    return parts


def halves(values):
    high = values.astype(jnp.bfloat16)
    low = (values - high.astype(jnp.float32)).astype(jnp.bfloat16)
    return high, low


def sketch_kernel(
    n_wide, n_narrow, cross, windows, n_chunks,
    bounds, gains, acts, cots, bits_in, left_ref, right_ref,
    out_ref, acts_all, bits_ref, flipped, table, bufs,
    local_sem, acts_send, acts_recv, cots_send, cots_recv,
):
    wide = lax.axis_index("wide")
    narrow = lax.axis_index("narrow")
    lines = n_wide // (2 * cross)
    core = lax.rem(wide, 2)
    side = lax.rem(wide // 2, cross)
    place = wide // (2 * cross)
    tok_acts = acts.shape[0]
    tok_cots = cots.shape[0]
    rows, cols = bits_in.shape
    row_block = left_ref.shape[0]
    col_block = right_ref.shape[0]
    row_groups = rows // row_block
    per_group = col_block // LANES
    seg_count = len(windows)
    stretch = per_group * rows * seg_count

    def index_of(at, across, on_core):
        return (at * cross + across) * 2 + on_core

    partner = index_of(place, side, 1 - core)
    up = index_of(lax.rem(place + 1, lines), side, core)
    down = index_of(lax.rem(place + lines - 1, lines), side, core)
    across = [lax.rem(side + off, cross) for off in range(1, cross)]
    has_up = place < lines - 1
    has_down = place > 0

    my_acts = pl.ds(narrow * tok_acts, tok_acts)
    my_cots = pl.ds(wide * tok_cots, tok_cots)

    def columns_of(chunk):
        return pl.ds(pl.multiple_of(chunk * col_block, col_block), col_block)

    def own_cots(chunk):
        return pltpu.make_async_copy(
            cots.at[:, columns_of(chunk)], bufs.at[chunk, my_cots, :], local_sem.at[2 + chunk]
        )

    def put_out(chunk):
        span = pl.ds(pl.multiple_of(chunk * stretch, 8), stretch)
        return pltpu.make_async_copy(
            table.at[span, :], out_ref.at[span, :], local_sem.at[2 + n_chunks + chunk]
        )

    own_acts = pltpu.make_async_copy(acts, acts_all.at[my_acts, :], local_sem.at[0])
    own_bits = pltpu.make_async_copy(bits_in, bits_ref, local_sem.at[1])
    for chunk in range(n_chunks):
        own_cots(chunk).start()
    own_acts.start()
    own_bits.start()

    barrier = pltpu.get_barrier_semaphore()

    def greet(**where):
        pl.semaphore_signal(barrier, inc=1, device_id=where, device_id_type=MESH)

    greet(wide=partner)
    for other in across:
        greet(wide=index_of(place, other, core))
    for off in range(1, n_narrow):
        greet(narrow=lax.rem(narrow + off, n_narrow))

    @pl.when(has_up)
    def _():
        greet(wide=up)

    @pl.when(has_down)
    def _():
        greet(wide=down)

    ends = jnp.where(has_up, 1, 0) + jnp.where(has_down, 1, 0)
    pl.semaphore_wait(barrier, 1 + (cross - 1) + (n_narrow - 1) + ends)

    def acts_copy(off):
        return pltpu.make_async_remote_copy(
            src_ref=acts,
            dst_ref=acts_all.at[my_acts, :],
            send_sem=acts_send.at[off],
            recv_sem=acts_recv.at[off],
            device_id={"narrow": lax.rem(narrow + off, n_narrow)},
            device_id_type=MESH,
        )

    def cots_copy(chunk, way, shard, to):
        place_of = bufs.at[chunk, pl.ds(shard * tok_cots, tok_cots), :]
        return pltpu.make_async_remote_copy(
            src_ref=place_of,
            dst_ref=place_of,
            send_sem=cots_send.at[way, chunk, shard],
            recv_sem=cots_recv.at[chunk, shard],
            device_id={"wide": to},
            device_id_type=MESH,
        )

    def outgoing(chunk, shard, climbs, drops, crosses):
        todo = []
        if climbs:
            todo.append((has_up, cots_copy(chunk, 0, shard, up)))
        if drops:
            todo.append((has_down, cots_copy(chunk, 1, shard, down)))
        if crosses:
            for at, other in enumerate(across):
                to = index_of(place, other, core)
                todo.append((None, cots_copy(chunk, 3 + at, shard, to)))
        todo.append((None, cots_copy(chunk, 2, shard, partner)))
        return todo

    def each(todo, act):
        for condition, copy in todo:
            if condition is None:
                act(copy)
            else:
                pl.when(condition)(functools.partial(act, copy))

    def start(copy):
        copy.start()

    def sent(copy):
        copy.wait_send()

    def arrived(chunk, shard):
        cots_copy(chunk, 2, shard, partner).wait_recv()

    def from_lines(chunk, step, act, wait):
        @pl.when(place - step >= 0)
        def _():
            shard = index_of(place - step, side, core)
            if wait:
                arrived(chunk, shard)
            each(outgoing(chunk, shard, True, False, True), act)

        @pl.when(place + step < lines)
        def _():
            shard = index_of(place + step, side, core)
            if wait:
                arrived(chunk, shard)
            each(outgoing(chunk, shard, False, True, True), act)

    def from_cross(chunk, step):
        for other in across:
            for sign in (1,) if step == 0 else (-1, 1):
                at = place + sign * step

                @pl.when((at >= 0) & (at < lines))
                def _():
                    shard = index_of(at, other, core)
                    arrived(chunk, shard)
                    each(outgoing(chunk, shard, False, False, False), start)

    def launch(chunk):
        own_cots(chunk).wait()
        each(outgoing(chunk, wide, True, True, True), start)

    def prepare():
        own_acts.wait()
        for off in range(1, n_narrow):
            acts_copy(off).wait()
        own_bits.wait()
        tile = 256
        offset = 0
        for seg, (low, high) in enumerate(windows):

            def one(at, _):
                begin = pl.multiple_of(low + at * tile, tile)
                values = acts_all[pl.ds(begin, tile), :].astype(jnp.float32)
                where_at = begin + lax.broadcasted_iota(jnp.int32, values.shape, 0)
                inside = (where_at >= bounds[0, seg]) & (where_at < bounds[1, seg])
                values = jnp.where(inside, values, 0.0)
                spot = pl.multiple_of(offset + at * tile, tile)
                flipped[:, pl.ds(spot, tile)] = values.T.astype(jnp.bfloat16)
                return 0

            lax.fori_loop(0, (high - low) // tile, one, 0)
            offset += high - low

    def compute(chunk):
        for at in range(lines):
            for over in range(cross):
                arrived(chunk, index_of(at, over, 1 - core))

        columns = columns_of(chunk)
        offset = 0
        for seg, (low, high) in enumerate(windows):
            grad = jnp.dot(
                flipped[:, offset : offset + high - low],
                bufs[chunk, low:high, :],
                preferred_element_type=jnp.float32,
            )
            offset += high - low
            sign = (1 - 2 * bits_ref[:, columns]).astype(jnp.float32)
            grad = grad * (sign * gains[seg])
            parts = [
                grad[group * row_block : (group + 1) * row_block]
                for group in range(row_groups)
            ]
            for group, part in enumerate(butterflies(parts)):
                upper, lower = halves(part)
                mixed = jnp.dot(
                    left_ref[...], upper, preferred_element_type=jnp.float32
                ) + jnp.dot(left_ref[...], lower, preferred_element_type=jnp.float32)
                upper, lower = halves(mixed)
                mixed = jnp.dot(
                    upper, right_ref[...], preferred_element_type=jnp.float32
                ) + jnp.dot(lower, right_ref[...], preferred_element_type=jnp.float32)
                for lane_block in range(per_group):
                    block = chunk * per_group + lane_block
                    base = (block * rows + group * row_block) * seg_count + seg
                    table[pl.ds(base, row_block, stride=seg_count), :] = mixed[
                        :, lane_block * LANES : (lane_block + 1) * LANES
                    ]
        put_out(chunk).start()

    launch(0)
    for off in range(1, n_narrow):
        acts_copy(off).start()

    def slot_work(slot, _):
        @pl.when(slot + 1 < n_chunks)
        def _():
            launch(slot + 1)

        for step in range(lines, 0, -1):
            chunk = slot + 1 - step

            @pl.when((chunk >= 0) & (chunk < n_chunks))
            def _():
                if step < lines:
                    from_lines(chunk, step, start, True)
                from_cross(chunk, step - 1)

        pl.when(slot == lines)(prepare)

        @pl.when(slot >= lines)
        def _():
            compute(slot - lines)

        return 0

    lax.fori_loop(0, n_chunks + lines, slot_work, 0)

    def finish(chunk, _):
        each(outgoing(chunk, wide, True, True, True), sent)
        for step in range(1, lines):
            from_lines(chunk, step, sent, False)
        for at in range(lines):
            for other in across:
                shard = index_of(at, other, core)
                each(outgoing(chunk, shard, False, False, False), sent)
        put_out(chunk).wait()
        return 0

    lax.fori_loop(0, n_chunks, finish, 0)


def pick_kernel(seg_count, n_chunks, spots, parts_ref, signs_ref, out_ref, table):
    stretch = parts_ref.shape[0] // n_chunks

    def join(at, _):
        base = pl.multiple_of(at * 8, 8)
        spans = [pl.ds(base + chunk * stretch, 8) for chunk in range(n_chunks)]
        parts = butterflies([parts_ref[span, :] for span in spans])
        for span, part in zip(spans, parts):
            table[span, :] = part
        return 0

    lax.fori_loop(0, stretch // 8, join, 0, unroll=2)

    lane = lax.broadcasted_iota(jnp.int32, (8, LANES), 1)
    chains = 4

    def pick(group, _):
        found = [jnp.zeros((8, LANES), jnp.float32)] * chains
        for at in range(LANES):
            spot = spots[group * LANES + at]
            values = table[pl.ds(lax.shift_right_logical(spot, 7), 8), :]
            values = pltpu.roll(values, spot & (LANES - 1), 1)
            found[at % chains] = jnp.where(lane == at, values, found[at % chains])
        both = (found[0] + found[1]) + (found[2] + found[3])
        out_ref[group] = both[:seg_count] * signs_ref[pl.ds(group, 1), :]
        return 0

    lax.fori_loop(0, out_ref.shape[0], pick, 0)


def local_sketch(acts, cots, bits, lengths, spots, signs, n_wide, n_narrow):
    tokens = acts.shape[0] * n_narrow
    rows, cols = bits.shape
    seg_count = lengths.shape[0]
    groups = signs.shape[0]
    cross = 2
    row_block, col_block = min(rows, 256), min(cols, 256)
    n_chunks = cols // col_block
    windows = []
    for seg in range(seg_count):
        low = max(0, tokens - (seg_count - seg) * MOST) // 256 * 256
        high = min(tokens, -(-(seg + 1) * MOST // 256) * 256)
        windows.append((low, high))
    ends = jnp.cumsum(lengths)
    bounds = jnp.stack([ends - lengths, ends]).astype(jnp.int32)
    gains = lax.rsqrt(lengths.astype(jnp.float32))
    anywhere = pl.BlockSpec(memory_space=pl.ANY)
    scalars = pl.BlockSpec(memory_space=pltpu.SMEM)
    vectors = pl.BlockSpec(memory_space=pltpu.VMEM)
    table = rows * cols // LANES * seg_count
    parts = pl.pallas_call(
        functools.partial(sketch_kernel, n_wide, n_narrow, cross, tuple(windows), n_chunks),
        out_shape=jax.ShapeDtypeStruct((table, LANES), jnp.float32),
        in_specs=[scalars] * 2 + [anywhere] * 3 + [vectors] * 2,
        out_specs=anywhere,
        scratch_shapes=[
            pltpu.VMEM((tokens, rows), acts.dtype),
            pltpu.VMEM((rows, cols), bits.dtype),
            pltpu.VMEM((rows, sum(high - low for low, high in windows)), jnp.bfloat16),
            pltpu.VMEM((table, LANES), jnp.float32),
            pltpu.VMEM((n_chunks, cots.shape[0] * n_wide, col_block), cots.dtype),
            pltpu.SemaphoreType.DMA((2 + 2 * n_chunks,)),
            pltpu.SemaphoreType.DMA((n_narrow,)),
            pltpu.SemaphoreType.DMA((n_narrow,)),
            pltpu.SemaphoreType.DMA((2 + cross, n_chunks, n_wide)),
            pltpu.SemaphoreType.DMA((n_chunks, n_wide)),
        ],
        compiler_params=pltpu.CompilerParams(
            collective_id=0, has_side_effects=True, vmem_limit_bytes=62 * 1024 * 1024
        ),
        name="local_sketch",
    )(bounds, gains, acts, cots, bits, sylvester(row_block), sylvester(col_block))
    return pl.pallas_call(
        functools.partial(pick_kernel, seg_count, n_chunks),
        out_shape=jax.ShapeDtypeStruct((groups, seg_count, LANES), jnp.float32),
        in_specs=[scalars, vectors, vectors],
        out_specs=vectors,
        scratch_shapes=[pltpu.VMEM((table + 8, LANES), jnp.float32)],
        compiler_params=pltpu.CompilerParams(vmem_limit_bytes=62 * 1024 * 1024),
        name="pick",
    )(spots, parts, signs)


def add_up_kernel(n_wide, n_narrow, shares, out, held, send_sem, recv_sem):
    count = n_wide * n_narrow
    me = lax.axis_index("wide") * n_narrow + lax.axis_index("narrow")
    barrier = pltpu.get_barrier_semaphore()

    def address(who):
        return {"wide": who // n_narrow, "narrow": lax.rem(who, n_narrow)}

    def greet(off, _):
        who = lax.rem(me + off, count)
        pl.semaphore_signal(barrier, inc=1, device_id=address(who), device_id_type=MESH)
        return 0

    lax.fori_loop(1, count, greet, 0)
    pl.semaphore_wait(barrier, count - 1)

    def copy_to(who, slot):
        return pltpu.make_async_remote_copy(
            src_ref=shares.at[who],
            dst_ref=held.at[slot],
            send_sem=send_sem.at[who],
            recv_sem=recv_sem.at[slot],
            device_id=address(who),
            device_id_type=MESH,
        )

    def send(off, _):
        copy_to(lax.rem(me + off, count), me).start()
        return 0

    lax.fori_loop(1, count, send, 0)
    out[...] = shares[me]

    def take(off, _):
        who = lax.rem(me + count - off, count)
        copy_to(who, who).wait_recv()
        out[...] += held[who]
        return 0

    lax.fori_loop(1, count, take, 0)

    def sent(off, _):
        copy_to(lax.rem(me + off, count), me).wait_send()
        return 0

    lax.fori_loop(1, count, sent, 0)


def add_up(shares, n_wide, n_narrow):
    count = n_wide * n_narrow
    in_vmem = pl.BlockSpec(memory_space=pltpu.VMEM)
    return pl.pallas_call(
        functools.partial(add_up_kernel, n_wide, n_narrow),
        out_shape=jax.ShapeDtypeStruct(shares.shape[1:], shares.dtype),
        in_specs=[in_vmem],
        out_specs=in_vmem,
        scratch_shapes=[
            pltpu.VMEM(shares.shape, shares.dtype),
            pltpu.SemaphoreType.DMA((count,)),
            pltpu.SemaphoreType.DMA((count,)),
        ],
        compiler_params=pltpu.CompilerParams(collective_id=1, has_side_effects=True),
        name="add_up",
    )(shares)


def body(n_wide, n_narrow, activations, cotangent, sign_bits, seg_lengths, kept_index):
    rows, cols = sign_bits.shape
    seg_count = seg_lengths.shape[0]
    kept = kept_index.shape[0]
    count = n_wide * n_narrow
    scale = 1.0 / math.sqrt(rows * n_wide * cols * n_narrow)
    full_cols = cols * n_narrow
    row_of = kept_index // full_cols
    col_of = kept_index % full_cols
    common = lax.population_count((row_of // rows) & lax.axis_index("wide"))
    common = common + lax.population_count((col_of // cols) & lax.axis_index("narrow"))
    signs = (1 - 2 * (common & 1)).astype(jnp.float32) * scale
    col = col_of % cols
    row = ((col // LANES) * rows + row_of % rows) * seg_count
    lane = jnp.arange(kept, dtype=jnp.int32)
    spots = row * LANES + ((lane - col) & (LANES - 1))
    shares = local_sketch(
        activations, cotangent, sign_bits, seg_lengths, spots, signs.reshape(-1, LANES),
        n_wide, n_narrow,
    )
    each = kept // count
    if each % LANES:
        flat = shares.transpose(1, 0, 2).reshape(seg_count, kept)
        return lax.psum_scatter(flat, ("wide", "narrow"), scatter_dimension=1, tiled=True)
    mine = add_up(shares.reshape(count, -1, LANES), n_wide, n_narrow)
    mine = mine.reshape(each // LANES, seg_count, LANES)
    return mine.transpose(1, 0, 2).reshape(seg_count, each)


def solution(mesh):
    return jax.shard_map(
        functools.partial(body, mesh.shape["wide"], mesh.shape["narrow"]),
        mesh=mesh,
        in_specs=(P("narrow", "wide"), P("wide", "narrow"), P("wide", "narrow"), P(), P()),
        out_specs=P(None, ("wide", "narrow")),
        check_vma=False,
    )
```

time: 834 us -> 200 us (0.24)
  local copies, waits for them, and re-layouts: 326 us -> 1.3 us
  matrix products: 215 us -> 0 us
  waiting for transfers between devices: 215 us -> 0 us
  Pallas kernels: 0 us -> 192 us
  other arithmetic: 50.3 us -> 6.46 us
  between operations: 13.2 us -> 0.02 us
  loops' own time: 9.46 us -> 0 us
    gather x3 -> x0, local copies, waits for them, and re-layouts: 294 us -> none  [the longest x1 185 us: body(): picked = jnp.take(mixed.reshape(seg_count, -1), local_flat, axis=1)]
    dot_general x6 -> x0, matrix products: 215 us -> none  [the longest x1 117 us: body(): jnp.einsum('sac,cd->sad', mixed, sylvester(cols_local), precision=highest)]
    pallas_call x0 -> x3, Pallas kernels: none -> 192 us  [the longest x1 139 us: local_sketch(): pl.pallas_call(functools.partial(sketch_kernel, n_wide, n_narrow, cross,...]
    unnamed x4 -> x0, waiting for transfers between devices: 183 us -> none
    all_gather x2 -> x0, waiting for transfers between devices: 32.2 us -> none  [the longest x1 32.2 us: body(): all_cots = lax.all_gather(cotangent, 'wide', axis=0, tiled=True)]
    unnamed x7 -> x1, local copies, waits for them, and re-layouts: 27.6 us -> 1.3 us
    dot_general x1 -> x0, other arithmetic: 26.2 us -> none  [body(): jnp.einsum('sac,cd->sad', mixed, sylvester(cols_local), precision=highest)]
    mul x2 -> x0, other arithmetic: 13.9 us -> none  [body(): picked = picked * (wide_sign * narrow_sign * scale)[None, :]]
  transfers between devices with their start and end apart: 3 -> 0, of which waited for: 2 -> 0; matrix products, arithmetic and copies ran while one was open for 19% -> 0% of each run, Pallas kernels for 0% -> 0%
where the time goes in v2:
time: 200 us; the launch traced here: 199 us
  Pallas kernels  192 us (96%)
  other arithmetic  6.46 us (3%)
    pallas_call x1, Pallas kernels, local_sketch(): pl.pallas_call(functools.partial(sketch_kernel, n_wide, n_narrow, cross,...  139 us
    pallas_call x1, Pallas kernels, local_sketch(): pl.pallas_call(functools.partial(pick_kernel, seg_count, n_chunks), out_s...  40.6 us
    pallas_call x1, Pallas kernels, add_up(): pl.pallas_call(functools.partial(add_up_kernel, n_wide, n_narrow), out_sh...  12.3 us

profile of v2, /device:TPU:0, one launch (start us, length us, event | category | flops | bytes accessed | tf_op | source)
XLA Modules:
  0.0 199.5 jit_solution(4328434830234079343)
XLA Ops:
  0.0 0.8 reduce-window.4
  0.8 0.7 fusion.23
  1.5 0.6 pad_add_fusion.bounds
  2.1 1.2 convert_rsqrt_fusion.gains
  3.2 1.6 fusion.13.signs_ref
  4.9 1.6 fusion.4.spots
  6.5 138.7 %local_sketch.1.parts_ref = f32[32768,128]{1,0:T(8,128)} custom-call(s32[2,4]{1,0:T(2,128)} %pad_add_fusion.bounds, f32[4]{0:T(128)} %convert_rsqrt_fusion.gains, bf16[2048,512]{1,0:T(8,128)(2,1)} %acts.1, bf16[256,2048]{1,0:T(8,128)(2,1)} %cots.1, s32[512,2048]{1,0:T(8,128)} %bits_in.1, bf16[256,256]{1,0:T(8,128)(2,1)} %constant.102.clone.left_ref.right_ref, ...), custom_call_target="tpu_custom_call" | custom-call | tf_op jit(solution)/shard_map/local_sketch/pallas_call | solution.py:353
  145.2 40.6 %pick.1 = f32[128,4,128]{2,1,0:T(4,128)} custom-call(s32[16384]{0:T(1024)} %fusion.4.spots, f32[32768,128]{1,0:T(8,128)} %local_sketch.1.parts_ref, f32[128,128]{1,0:T(8,128)} %fusion.13.signs_ref), custom_call_target="tpu_custom_call" | custom-call | tf_op jit(solution)/shard_map/pick/pallas_call | solution.py:375
  185.9 12.3 %add_up.1 = f32[16,128]{1,0:T(8,128)} custom-call(f32[32,16,128]{2,1,0:T(8,128)} %bitcast.16), custom_call_target="tpu_custom_call" | custom-call | tf_op jit(solution)/shard_map/add_up/pallas_call | solution.py:437
  198.2 1.3 copy.10

commit v3 on v2

--- a/solution.py
+++ b/solution.py
@@ -276,15 +276,15 @@
                     from_lines(chunk, step, start, True)
                 from_cross(chunk, step - 1)
 
-        pl.when(slot == lines)(prepare)
-
-        @pl.when(slot >= lines)
+        pl.when(slot == lines + 1)(prepare)
+
+        @pl.when(slot >= lines + 1)
         def _():
-            compute(slot - lines)
-
-        return 0
-
-    lax.fori_loop(0, n_chunks + lines, slot_work, 0)
+            compute(slot - lines - 1)
+
+        return 0
+
+    lax.fori_loop(0, n_chunks + lines + 1, slot_work, 0)
 
     def finish(chunk, _):
         each(outgoing(chunk, wide, True, True, True), sent)

time: 200 us -> 207 us (1.035)
  Pallas kernels: 192 us -> 199 us
    pallas_call x1, Pallas kernels: 139 us -> 143 us  [local_sketch(): pl.pallas_call(functools.partial(sketch_kernel, n_wide, n_narrow, cross,...]
    pallas_call x1, Pallas kernels: 12.3 us -> 15.9 us  [add_up(): pl.pallas_call(functools.partial(add_up_kernel, n_wide, n_narrow), out_sh...]
where the time goes in v3:
time: 207 us
  Pallas kernels  199 us (96%)
  other arithmetic  6.46 us (3%)
    pallas_call x1, Pallas kernels, local_sketch(): pl.pallas_call(functools.partial(sketch_kernel, n_wide, n_narrow, cross,...  143 us
    pallas_call x1, Pallas kernels, local_sketch(): pl.pallas_call(functools.partial(pick_kernel, seg_count, n_chunks), out_s...  40.6 us
    pallas_call x1, Pallas kernels, add_up(): pl.pallas_call(functools.partial(add_up_kernel, n_wide, n_narrow), out_sh...  15.9 us

profile of v3, /device:TPU:0, one launch (start us, length us, event | category | flops | bytes accessed | tf_op | source)
XLA Modules:
  0.0 207.1 jit_solution(5142239878637248080)
XLA Ops:
  0.0 0.8 reduce-window.4
  0.8 0.7 fusion.23
  1.5 0.6 pad_add_fusion.bounds
  2.1 1.2 convert_rsqrt_fusion.gains
  3.2 1.6 fusion.13.signs_ref
  4.9 1.6 fusion.4.spots
  6.5 142.8 %local_sketch.1.parts_ref = f32[32768,128]{1,0:T(8,128)} custom-call(s32[2,4]{1,0:T(2,128)} %pad_add_fusion.bounds, f32[4]{0:T(128)} %convert_rsqrt_fusion.gains, bf16[2048,512]{1,0:T(8,128)(2,1)} %acts.1, bf16[256,2048]{1,0:T(8,128)(2,1)} %cots.1, s32[512,2048]{1,0:T(8,128)} %bits_in.1, bf16[256,256]{1,0:T(8,128)(2,1)} %constant.102.clone.left_ref.right_ref, ...), custom_call_target="tpu_custom_call" | custom-call | tf_op jit(solution)/shard_map/local_sketch/pallas_call | solution.py:353
  149.3 40.6 %pick.1 = f32[128,4,128]{2,1,0:T(4,128)} custom-call(s32[16384]{0:T(1024)} %fusion.4.spots, f32[32768,128]{1,0:T(8,128)} %local_sketch.1.parts_ref, f32[128,128]{1,0:T(8,128)} %fusion.13.signs_ref), custom_call_target="tpu_custom_call" | custom-call | tf_op jit(solution)/shard_map/pick/pallas_call | solution.py:375
  189.9 15.9 %add_up.1 = f32[16,128]{1,0:T(8,128)} custom-call(f32[32,16,128]{2,1,0:T(8,128)} %bitcast.16), custom_call_target="tpu_custom_call" | custom-call | tf_op jit(solution)/shard_map/add_up/pallas_call | solution.py:437
  205.8 1.3 copy.10
